TPU v7x, 128 devices: a whole 4x4x4 slice. The times are simulated.
128 devices in a mesh: dom: 128 (over x, y, z, core).
Axes of the slice: x: 4, y: 4, z: 4, core: 2. Of those that a mesh axis runs over, the one named last changes fastest.
Arguments:
- traction: float32 [65536, 3, 128], P('dom'), may hold values from -6 to 6
- fluid_coords: float32 [65536, 3, 128], P('dom'), may hold values from 0 to 1
- struct_coords: float32 [3, 32, 16384], P(None, None, 'dom'), may hold values from 0 to 1
- dest: int32 [65536, 1], P('dom'), may hold values from 0 to 127; in each aligned block of 512 rows (0 to 511, 512 to 1023, ...) at most 8 rows name the same one
- target: int32 [65536], P('dom'), may hold values from 0 to 127
- blocks: float32 [3, 96, 96, 16384], P(None, None, None, 'dom'), may hold values from -1 to 7, as said below
- columns: int32 [2, 16384], P(None, 'dom'), may hold values from 0 to 159
- halo_list: int32 [2048], P('dom'), may hold values from 0 to 127
- precond: float32 [96, 96, 16384], P(None, None, 'dom'), may hold values from -1 to 1
Outputs:
- load_field: float32 [96, 16384], P(None, 'dom')
- solution: float32 [96, 16384], P(None, 'dom')
- residual: float32 [96, 16384], P(None, 'dom')
Inputs may be any that keep to these rules, and one draw needn't show every extreme that they name: `dest`: among the fluid blocks of one partition no partition is named more than 8 times, a bound that some block reaches. Each diagonal block is its positive diagonal plus small full entries; coupling blocks are small full blocks.
All inputs are finite; a program needn't handle non-finite values.
Results may differ from a plain program's by a relative error of at most 0.0003.
Values sent between devices are 32-bit elements; how exact they have to be, the bound alone decides.
No kernel may reach another device: no remote copies, remote signals or barrier semaphores. Data moves between devices by JAX's collectives and lax.ppermute only.
A program may use at most 128 MiB of HBM per device.

v0:
```python
import jax
import jax.numpy as jnp
from jax import lax
from jax.sharding import Mesh
from jax.sharding import PartitionSpec as P

ITERS = 2
DOM = ("dom_0", "dom_1", "dom_2", "dom_3")
support = 0.9


def from_behind(block, axis, distance):
    devices = range(lax.axis_size(axis))
    route = [(i - distance, i) for i in devices if i - distance in devices]
    return lax.ppermute(block, axis, route)


def over_axes(shard, axes):
    for axis in axes:
        shard = lax.psum(shard, axis)
    return shard


def wendland_map(fluid_pos, force, struct_pos):
    dist_sq = jnp.zeros((fluid_pos.shape[0], struct_pos.shape[2], fluid_pos.shape[2]), jnp.float32)
    for component in range(3):
        dist_sq = (
            dist_sq + (struct_pos[:, component, :, None] - fluid_pos[:, component, None, :]) ** 2
        )
    radius = jnp.sqrt(dist_sq) / support
    weight = jnp.maximum(1.0 - radius, 0.0) ** 4 * (4.0 * radius + 1.0)
    mapped = jnp.einsum("bjn,bcn->bcj", weight, force, precision=lax.Precision.HIGHEST)
    return mapped.reshape(mapped.shape[0], -1)


def precondition(precond, vector):
    return jnp.einsum("abi,bi->ai", precond, vector, precision=lax.Precision.HIGHEST)


def apply_operator(vector, blocks, columns, halo_list):
    outgoing = jnp.take(vector, halo_list, axis=1)
    from_left = from_behind(outgoing, DOM, 1)
    from_right = from_behind(outgoing, DOM, -1)
    extended = jnp.concatenate([vector, from_left, from_right], axis=1)
    result = jnp.einsum("abi,bi->ai", blocks[0], vector, precision=lax.Precision.HIGHEST)
    for neighbor in range(columns.shape[0]):
        taken = jnp.take(extended, columns[neighbor], axis=1)
        result = result + jnp.einsum(
            "abi,bi->ai", blocks[neighbor + 1], taken, precision=lax.Precision.HIGHEST
        )
    return result


def on_device(
    traction, fluid_coords, struct_coords, dest, target, blocks, columns, halo_list, precond
):
    partitions = lax.axis_size(DOM)
    fluid_count = dest.shape[0]
    node_count = traction.shape[2]
    cluster = blocks.shape[1]
    local_blocks = blocks.shape[3]
    capacity = max(2, 2 * fluid_count // partitions)
    owner_part = dest[:, 0]
    owner_hits = (owner_part[:, None] == jnp.arange(partitions, dtype=jnp.int32)[None, :]).astype(
        jnp.int32
    )
    before = jnp.sum((jnp.cumsum(owner_hits, axis=0) - owner_hits) * owner_hits, axis=1)
    slot_index = owner_part * capacity + before
    slot_target = jnp.zeros((partitions * capacity,), jnp.int32).at[slot_index].set(target)
    slot_target = slot_target.reshape(partitions, capacity)
    packed = jnp.concatenate([traction, fluid_coords], axis=1)
    outgoing = (
        jnp.zeros((partitions * capacity, 6, node_count), jnp.float32).at[slot_index].set(packed)
    )
    outgoing = outgoing.reshape(partitions, capacity, 6, node_count)
    floats = lax.all_to_all(outgoing, DOM, split_axis=0, concat_axis=0, tiled=True)
    labels = lax.all_to_all(slot_target, DOM, split_axis=0, concat_axis=0, tiled=True)
    item_count = floats.shape[1]
    flattened = floats.reshape(partitions * item_count, 6, node_count)
    struct_pos = jnp.transpose(jnp.take(struct_coords, labels.reshape(-1), axis=2), (2, 0, 1))
    mapped = wendland_map(flattened[:, 3:], flattened[:, :3], struct_pos)
    arrived, labels = (mapped.reshape(partitions, item_count, cluster), labels)
    onehot = (
        labels.reshape(-1)[:, None] == jnp.arange(local_blocks, dtype=jnp.int32)[None, :]
    ).astype(jnp.float32)
    load_field = jnp.dot(
        arrived.reshape(-1, cluster).T,
        onehot,
        precision=lax.Precision.HIGHEST,
        preferred_element_type=jnp.float32,
    )
    solution = jnp.zeros_like(load_field)
    residual = load_field
    search = load_field
    alignment = over_axes(jnp.sum(load_field * residual), DOM)
    for step in range(ITERS):
        search_pre = precondition(precond, search)
        image = apply_operator(search_pre, blocks, columns, halo_list)
        step_size = alignment / over_axes(jnp.sum(load_field * image), DOM)
        middle = residual - step_size * image
        middle_pre = precondition(precond, middle)
        middle_image = apply_operator(middle_pre, blocks, columns, halo_list)
        crossed, squared, with_middle, with_image = (
            over_axes(jnp.sum(middle_image * middle), DOM),
            over_axes(jnp.sum(middle_image * middle_image), DOM),
            over_axes(jnp.sum(load_field * middle), DOM),
            over_axes(jnp.sum(load_field * middle_image), DOM),
        )
        smoothing = crossed / squared
        solution = solution + step_size * search_pre + smoothing * middle_pre
        residual = middle - smoothing * middle_image
        new_alignment = with_middle - smoothing * with_image
        momentum = new_alignment / alignment * (step_size / smoothing)
        search = residual + momentum * (search - smoothing * image)
        alignment = new_alignment
    return (load_field, solution, residual)


def solution(mesh):
    finer = Mesh(mesh.devices.reshape(4, 4, 4, 2), ("dom_0", "dom_1", "dom_2", "dom_3"))
    in_specs = (
        P(DOM, None, None),
        P(DOM, None, None),
        P(None, None, DOM),
        P(DOM, None),
        P(DOM),
        P(None, None, None, DOM),
        P(None, DOM),
        P(DOM),
        P(None, None, DOM),
    )
    out_specs = (P(None, DOM), P(None, DOM), P(None, DOM))
    return jax.shard_map(
        on_device, mesh=finer, in_specs=in_specs, out_specs=out_specs, check_vma=False
    )
```

profile of v0, /device:TPU:1, one launch (start us, length us, event | category | flops | bytes accessed | tf_op | source)
XLA Modules:
  0.0 407.8 jit_solution(7936706679427344915)
XLA Ops:
  6.7 11.5 %all-to-all-start.1 = ((s32[128,1,8]{2,1,0:T(1,128)}), s32[128,1,8]{2,1,0:T(1,128)S(1)}, u32[]{:S(2)}, u32[]{:S(2)}) async-start(s32[128,1,8]{2,1,0:T(1,128)} %bitcast.41), calls=%async_computation.1 | async-start | bytes 131072 | tf_op jit(solution)/shard_map/all_to_all | solution.py:77
  22.8 47.3 %scatter_fusion = f32[1024,6,128]{2,1,0:T(8,128)} fusion(f32[1024,6,128]{2,1,0:T(8,128)} %broadcast_in_dim.40, s32[512]{0:T(512)S(1)} %bitcast.249, f32[512,6,128]{2,1,0:T(8,128)S(1)} %copy.103), kind=kCustom, calls=%fused_computation.13 | custom fusion | bytes 4720640 | tf_op jit(solution)/shard_map/scatter | solution.py:73
  74.7 9.8 %all-to-all-start = ((f32[128,8,6,128]{3,1,2,0:T(8,128)}), f32[128,8,6,128]{3,1,2,0:T(8,128)S(1)}, u32[]{:S(2)}, u32[]{:S(2)}) async-start(f32[128,8,6,128]{3,1,2,0:T(8,128)} %copy.104), calls=%async_computation | async-start | bytes 6291456 | tf_op jit(solution)/shard_map/all_to_all | solution.py:76
  87.8 8.0 %gather_fusion = f32[1024,3,32]{2,1,0:T(4,128)} fusion(f32[3,32,128]{1,0,2:T(4,128)S(1)} %copy.107, s32[1024]{0:T(1024)S(1)} %broadcast_clamp_fusion), kind=kCustom, calls=%fused_computation.12 | custom fusion | bytes 790528 | tf_op jit(solution)/shard_map/jit(_take)/gather | solution.py:80
  103.6 22.7 %all-to-all-done = f32[128,8,6,128]{3,1,2,0:T(8,128)S(1)} async-done(((f32[128,8,6,128]{3,1,2,0:T(8,128)}), f32[128,8,6,128]{3,1,2,0:T(8,128)S(1)}, u32[]{:S(2)}, u32[]{:S(2)}) %all-to-all-start) | async-done | bytes 3145760 | tf_op jit(solution)/shard_map/all_to_all | solution.py:76
  128.5 42.6 %fusion = f32[1024,3,32]{2,1,0:T(4,128)S(1)} fusion(f32[1024,128]{1,0:T(8,128)S(1)} %bitcast.242, f32[1024,32]{1,0:T(8,128)S(1)} %bitcast.240, f32[1024,128]{1,0:T(8,128)S(1)} %bitcast.243, f32[1024,32]{1,0:T(8,128)S(1)} %bitcast.239, f32[1024,128]{1,0:T(8,128)S(1)} %bitcast.241, f32[1024,32]{1,0:T(8,128)S(1)} %bitcast.238, f32[1024,6,128]{2,1,0:T(8,128)S(1)} %bitcast.223), kind=kOutput, calls=%fused_computation.15 | convolution fusion | flops 218103808 | bytes 5636096 | tf_op jit(solution)/shard_map/bjn,bcn->bcj/dot_general | solution.py:32
  184.4 6.2 %fusion.32 = (f32[128,96]{0,1:T(8,128)S(1)}, f32[128,96]{0,1:T(8,128)S(1)}, f32[128,96]{0,1:T(8,128)S(1)}) fusion(f32[3,96,96,128]{3,2,1,0:T(8,128)} %param.18, f32[128,96]{0,1:T(8,128)S(1)} %copy.236, f32[128,96]{0,1:T(8,128)S(1)} %multiply_reduce_fusion.3, f32[128,96]{0,1:T(8,128)S(1)} %copy.237), kind=kLoop, calls=%fused_computation.55 | loop fusion | flops 7041024 | bytes 14450688 | tf_op jit(solution)/shard_map/abi,bi->ai/dot_general | solution.py:48
  191.2 8.0 %all-reduce.8 = (f32[]{:T(128)}, f32[]{:T(128)}) all-reduce(f32[]{:T(128)} %get-tuple-element.24, f32[]{:T(128)} %get-tuple-element.23), channel_id=1, replica_groups=mesh['dom_0'=4,'dom_1'=4,'dom_2'=4,'dom_3'=2] {'dom_0'}, use_global_device_ids=true, to_apply=%region_6.7 | all-reduce | flops 2 | bytes 16 | tf_op jit(solution)/shard_map/psum | solution.py:20
  199.2 6.7 %all-reduce.5 = (f32[]{:T(128)}, f32[]{:T(128)}) all-reduce(f32[]{:T(128)} %get-tuple-element.47, f32[]{:T(128)} %get-tuple-element.48), channel_id=1, replica_groups=mesh['dom_0'=4,'dom_1'=4,'dom_2'=4,'dom_3'=2] {'dom_1'}, use_global_device_ids=true, to_apply=%region_7.8 | all-reduce | flops 2 | bytes 16 | tf_op jit(solution)/shard_map/psum | solution.py:20
  205.9 11.0 %all-reduce.2 = (f32[]{:T(128)}, f32[]{:T(128)}) all-reduce(f32[]{:T(128)} %get-tuple-element.39, f32[]{:T(128)} %get-tuple-element.40), channel_id=1, replica_groups=mesh['dom_0'=4,'dom_1'=4,'dom_2'=4,'dom_3'=2] {'dom_2'}, use_global_device_ids=true, to_apply=%region_8.9 | all-reduce | flops 2 | bytes 16 | tf_op jit(solution)/shard_map/psum | solution.py:20
  216.9 10.4 %all-reduce.11 = (f32[]{:T(128)}, f32[]{:T(128)}) all-reduce(f32[]{:T(128)} %get-tuple-element.31, f32[]{:T(128)} %get-tuple-element.32), channel_id=1, replica_groups=mesh['dom_0'=4,'dom_1'=4,'dom_2'=4,'dom_3'=2] {'dom_3'}, use_global_device_ids=true, to_apply=%region_9.10 | all-reduce | flops 2 | bytes 16 | tf_op jit(solution)/shard_map/psum | solution.py:20
  241.0 6.2 %fusion.33 = (f32[128,96]{0,1:T(8,128)S(1)}, f32[128,96]{0,1:T(8,128)S(1)}, f32[128,96]{0,1:T(8,128)S(1)}) fusion(f32[3,96,96,128]{3,2,1,0:T(8,128)} %param.18, f32[128,96]{0,1:T(8,128)S(1)} %copy.241, f32[128,96]{0,1:T(8,128)S(1)} %multiply_reduce_fusion.2, f32[128,96]{0,1:T(8,128)S(1)} %copy.242), kind=kLoop, calls=%fused_computation.56 | loop fusion | flops 7041024 | bytes 14450688 | tf_op jit(solution)/shard_map/abi,bi->ai/dot_general | solution.py:48
  248.0 9.3 %all-reduce.7 = (f32[]{:T(128)}, f32[]{:T(128)}, f32[]{:T(128)}, f32[]{:T(128)}) all-reduce(f32[]{:T(128)} %get-tuple-element.19, f32[]{:T(128)} %get-tuple-element.18, f32[]{:T(128)} %get-tuple-element.22, f32[]{:T(128)} %get-tuple-element.17), channel_id=1, replica_groups=mesh['dom_0'=4,'dom_1'=4,'dom_2'=4,'dom_3'=2] {'dom_0'}, use_global_device_ids=true, to_apply=%region_26.29 | all-reduce | flops 4 | bytes 32 | tf_op jit(solution)/shard_map/psum | solution.py:20
  257.3 6.7 %all-reduce.4 = (f32[]{:T(128)}, f32[]{:T(128)}, f32[]{:T(128)}, f32[]{:T(128)}) all-reduce(f32[]{:T(128)} %get-tuple-element.43, f32[]{:T(128)} %get-tuple-element.44, f32[]{:T(128)} %get-tuple-element.45, f32[]{:T(128)} %get-tuple-element.46), channel_id=1, replica_groups=mesh['dom_0'=4,'dom_1'=4,'dom_2'=4,'dom_3'=2] {'dom_1'}, use_global_device_ids=true, to_apply=%region_27.30 | all-reduce | flops 4 | bytes 32 | tf_op jit(solution)/shard_map/psum | solution.py:20
  264.0 11.5 %all-reduce.1 = (f32[]{:T(128)}, f32[]{:T(128)}, f32[]{:T(128)}, f32[]{:T(128)}) all-reduce(f32[]{:T(128)} %get-tuple-element.35, f32[]{:T(128)} %get-tuple-element.36, f32[]{:T(128)} %get-tuple-element.37, f32[]{:T(128)} %get-tuple-element.38), channel_id=1, replica_groups=mesh['dom_0'=4,'dom_1'=4,'dom_2'=4,'dom_3'=2] {'dom_2'}, use_global_device_ids=true, to_apply=%region_28.31 | all-reduce | flops 4 | bytes 32 | tf_op jit(solution)/shard_map/psum | solution.py:20
  275.5 10.1 %all-reduce.10 = (f32[]{:T(128)}, f32[]{:T(128)}, f32[]{:T(128)}, f32[]{:T(128)}) all-reduce(f32[]{:T(128)} %get-tuple-element.27, f32[]{:T(128)} %get-tuple-element.28, f32[]{:T(128)} %get-tuple-element.29, f32[]{:T(128)} %get-tuple-element.30), channel_id=1, replica_groups=mesh['dom_0'=4,'dom_1'=4,'dom_2'=4,'dom_3'=2] {'dom_3'}, use_global_device_ids=true, to_apply=%region_29.32 | all-reduce | flops 4 | bytes 32 | tf_op jit(solution)/shard_map/psum | solution.py:20
  310.6 9.3 %psum.276 = f32[]{:T(128)} all-reduce(f32[]{:T(128)} %fusion.51), channel_id=1, replica_groups=mesh['dom_0'=4,'dom_1'=4,'dom_2'=4,'dom_3'=2] {'dom_0'}, use_global_device_ids=true, to_apply=%region_36.39 | all-reduce | flops 1 | bytes 8 | tf_op jit(solution)/shard_map/psum | solution.py:20
  319.9 6.6 %psum.277 = f32[]{:T(128)} all-reduce(f32[]{:T(128)} %psum.276), channel_id=1, replica_groups=mesh['dom_0'=4,'dom_1'=4,'dom_2'=4,'dom_3'=2] {'dom_1'}, use_global_device_ids=true, to_apply=%region_37.40 | all-reduce | flops 1 | bytes 8 | tf_op jit(solution)/shard_map/psum | solution.py:20
  326.5 11.4 %psum.278 = f32[]{:T(128)} all-reduce(f32[]{:T(128)} %psum.277), channel_id=1, replica_groups=mesh['dom_0'=4,'dom_1'=4,'dom_2'=4,'dom_3'=2] {'dom_2'}, use_global_device_ids=true, to_apply=%region_38.41 | all-reduce | flops 1 | bytes 8 | tf_op jit(solution)/shard_map/psum | solution.py:20
  337.9 10.0 %psum.279 = f32[]{:T(128)} all-reduce(f32[]{:T(128)} %psum.278), channel_id=1, replica_groups=mesh['dom_0'=4,'dom_1'=4,'dom_2'=4,'dom_3'=2] {'dom_3'}, use_global_device_ids=true, to_apply=%region_39.42 | all-reduce | flops 1 | bytes 8 | tf_op jit(solution)/shard_map/psum | solution.py:20
  367.8 9.3 %all-reduce.6 = (f32[]{:T(128)}, f32[]{:T(128)}) all-reduce(f32[]{:T(128)} %get-tuple-element.21, f32[]{:T(128)} %get-tuple-element.20), channel_id=1, replica_groups=mesh['dom_0'=4,'dom_1'=4,'dom_2'=4,'dom_3'=2] {'dom_0'}, use_global_device_ids=true, to_apply=%region_41.44 | all-reduce | flops 2 | bytes 16 | tf_op jit(solution)/shard_map/psum | solution.py:20
  377.1 6.6 %all-reduce.3 = (f32[]{:T(128)}, f32[]{:T(128)}) all-reduce(f32[]{:T(128)} %get-tuple-element.41, f32[]{:T(128)} %get-tuple-element.42), channel_id=1, replica_groups=mesh['dom_0'=4,'dom_1'=4,'dom_2'=4,'dom_3'=2] {'dom_1'}, use_global_device_ids=true, to_apply=%region_42.45 | all-reduce | flops 2 | bytes 16 | tf_op jit(solution)/shard_map/psum | solution.py:20
  383.7 11.4 %all-reduce = (f32[]{:T(128)}, f32[]{:T(128)}) all-reduce(f32[]{:T(128)} %get-tuple-element.33, f32[]{:T(128)} %get-tuple-element.34), channel_id=1, replica_groups=mesh['dom_0'=4,'dom_1'=4,'dom_2'=4,'dom_3'=2] {'dom_2'}, use_global_device_ids=true, to_apply=%region_43.46 | all-reduce | flops 2 | bytes 16 | tf_op jit(solution)/shard_map/psum | solution.py:20
  395.1 10.0 %all-reduce.9 = (f32[]{:T(128)}, f32[]{:T(128)}) all-reduce(f32[]{:T(128)} %get-tuple-element.25, f32[]{:T(128)} %get-tuple-element.26), channel_id=1, replica_groups=mesh['dom_0'=4,'dom_1'=4,'dom_2'=4,'dom_3'=2] {'dom_3'}, use_global_device_ids=true, to_apply=%region_44.47 | all-reduce | flops 2 | bytes 16 | tf_op jit(solution)/shard_map/psum | solution.py:20
  (133 shorter events, 94.6 us)
Async XLA Ops:
  6.7 68.0 %all-to-all-start.1 = ((s32[128,1,8]{2,1,0:T(1,128)}), s32[128,1,8]{2,1,0:T(1,128)S(1)}, u32[]{:S(2)}, u32[]{:S(2)}) async-start(s32[128,1,8]{2,1,0:T(1,128)} %bitcast.41), calls=%async_computation.1 | async-start | bytes 131072 | tf_op jit(solution)/shard_map/all_to_all | solution.py:77
  74.7 9.9 %copy-start.4 = (f32[3,32,128]{2,1,0:T(8,128)S(1)}, f32[3,32,128]{2,1,0:T(8,128)}, u32[]{:S(2)}) copy-start(f32[3,32,128]{2,1,0:T(8,128)} %param.15) | copy-start | bytes 147460
  74.7 10.0 %copy-start.6 = (s32[16]{0:T(128)S(1)}, s32[16]{0:T(128)}, u32[]{:S(2)}) copy-start(s32[16]{0:T(128)} %param.20) | copy-start | bytes 196
  74.7 10.1 %copy-start.5 = (s32[2,128]{1,0:T(2,128)S(1)}, s32[2,128]{1,0:T(2,128)}, u32[]{:S(2)}) copy-start(s32[2,128]{1,0:T(2,128)} %param.19) | copy-start | bytes 3076
  74.7 51.6 %all-to-all-start = ((f32[128,8,6,128]{3,1,2,0:T(8,128)}), f32[128,8,6,128]{3,1,2,0:T(8,128)S(1)}, u32[]{:S(2)}, u32[]{:S(2)}) async-start(f32[128,8,6,128]{3,1,2,0:T(8,128)} %copy.104), calls=%async_computation | async-start | bytes 6291456 | tf_op jit(solution)/shard_map/all_to_all | solution.py:76
  126.3 2.2 copy-start.1
  126.3 2.2 copy-start.2
  126.3 2.2 copy-start.3
  172.2 176.4 %copy-start = (f32[96,128]{1,0:T(8,128)}, f32[96,128]{1,0:T(8,128)S(1)}, u32[]{:S(2)}) copy-start(f32[96,128]{1,0:T(8,128)S(1)} %fusion.41) | copy-start | bytes 147460
  176.1 5.6 %collective-permute-start.1 = (f32[96,16]{0,1:T(8,128)S(1)}, f32[96,16]{0,1:T(8,128)S(1)}, u32[]{:S(2)}, u32[]{:S(2)}) collective-permute-start(f32[96,16]{0,1:T(8,128)S(1)} %select_bitcast_fusion.3), channel_id=1, source_target_pairs={{1,0},{2,1},{3,2},{4,3},{5,4},{6,5},{7,6},{8,7},{9,8},{10,9},{11,1... | collective-permute-start | bytes 18440 | tf_op jit(solution)/shard_map/ppermute | solution.py:15
  179.2 3.3 collective-permute-start
  232.5 6.0 %collective-permute-start.3 = (f32[96,16]{0,1:T(8,128)S(1)}, f32[96,16]{0,1:T(8,128)S(1)}, u32[]{:S(2)}, u32[]{:S(2)}) collective-permute-start(f32[96,16]{0,1:T(8,128)S(1)} %select_bitcast_fusion.2), channel_id=1, source_target_pairs={{1,0},{2,1},{3,2},{4,3},{5,4},{6,5},{7,6},{8,7},{9,8},{10,9},{11,1... | collective-permute-start | bytes 18440 | tf_op jit(solution)/shard_map/ppermute | solution.py:15
  234.8 4.3 %collective-permute-start.2 = (f32[96,16]{0,1:T(8,128)S(1)}, f32[96,16]{0,1:T(8,128)S(1)}, u32[]{:S(2)}, u32[]{:S(2)}) collective-permute-start(f32[96,16]{0,1:T(8,128)S(1)} %select_bitcast_fusion.2), channel_id=1, source_target_pairs={{0,1},{1,2},{2,3},{3,4},{4,5},{5,6},{6,7},{7,8},{8,9},{9,10},{10,1... | collective-permute-start | bytes 18440 | tf_op jit(solution)/shard_map/ppermute | solution.py:15
  295.2 5.8 %collective-permute-start.5 = (f32[96,16]{0,1:T(8,128)S(1)}, f32[96,16]{0,1:T(8,128)S(1)}, u32[]{:S(2)}, u32[]{:S(2)}) collective-permute-start(f32[96,16]{0,1:T(8,128)S(1)} %select_bitcast_fusion.1), channel_id=1, source_target_pairs={{1,0},{2,1},{3,2},{4,3},{5,4},{6,5},{7,6},{8,7},{9,8},{10,9},{11,1... | collective-permute-start | bytes 18440 | tf_op jit(solution)/shard_map/ppermute | solution.py:15
  297.5 4.3 %collective-permute-start.4 = (f32[96,16]{0,1:T(8,128)S(1)}, f32[96,16]{0,1:T(8,128)S(1)}, u32[]{:S(2)}, u32[]{:S(2)}) collective-permute-start(f32[96,16]{0,1:T(8,128)S(1)} %select_bitcast_fusion.1), channel_id=1, source_target_pairs={{0,1},{1,2},{2,3},{3,4},{4,5},{5,6},{6,7},{7,8},{8,9},{9,10},{10,1... | collective-permute-start | bytes 18440 | tf_op jit(solution)/shard_map/ppermute | solution.py:15
  352.5 5.8 %collective-permute-start.7 = (f32[96,16]{0,1:T(8,128)S(1)}, f32[96,16]{0,1:T(8,128)S(1)}, u32[]{:S(2)}, u32[]{:S(2)}) collective-permute-start(f32[96,16]{0,1:T(8,128)S(1)} %select_bitcast_fusion), channel_id=1, source_target_pairs={{1,0},{2,1},{3,2},{4,3},{5,4},{6,5},{7,6},{8,7},{9,8},{10,9},{11,1... | collective-permute-start | bytes 18440 | tf_op jit(solution)/shard_map/ppermute | solution.py:15
  354.8 4.3 %collective-permute-start.6 = (f32[96,16]{0,1:T(8,128)S(1)}, f32[96,16]{0,1:T(8,128)S(1)}, u32[]{:S(2)}, u32[]{:S(2)}) collective-permute-start(f32[96,16]{0,1:T(8,128)S(1)} %select_bitcast_fusion), channel_id=1, source_target_pairs={{0,1},{1,2},{2,3},{3,4},{4,5},{5,6},{6,7},{7,8},{8,9},{9,10},{10,1... | collective-permute-start | bytes 18440 | tf_op jit(solution)/shard_map/ppermute | solution.py:15
where the time goes:
time: 410 us; the launch traced here: 408 us
  blocking collectives  148 us (36%)
  local copies, waits for them, and re-layouts  83.5 us (20%)
  other arithmetic  52.8 us (13%)
  starting transfers between devices  44.4 us (11%)
  matrix products  43.1 us (11%)
  waiting for transfers between devices  25.2 us (6%)
  between operations  10.3 us (3%)
    psum x16, blocking collectives, over_axes(): shard = lax.psum(shard, axis)  148 us
    scatter x1, local copies, waits for them, and re-layouts, on_device(): jnp.zeros((partitions * capacity, 6, node_count), jnp.float32)  47.3 us
    dot_general x1, matrix products, wendland_map(): jnp.einsum('bjn,bcn->bcj', weight, force, precision=lax.Precision.HIGHEST)  42.6 us
    dot_general x4, other arithmetic, apply_operator(): jnp.einsum('abi,bi->ai', blocks[neighbor + 1], taken, precision=lax.Preci...  24.9 us
    ppermute x8, starting transfers between devices, from_behind(): return lax.ppermute(block, axis, route)  23.1 us
    all_to_all x1, waiting for transfers between devices, on_device(): lax.all_to_all(outgoing, DOM, split_axis=0, concat_axis=0, tiled=True)  22.7 us
    dot_general x4, other arithmetic, precondition(): jnp.einsum('abi,bi->ai', precond, vector, precision=lax.Precision.HIGHEST)  12.5 us
    all_to_all x1, starting transfers between devices, on_device(): lax.all_to_all(slot_target, DOM, split_axis=0, concat_axis=0, tiled=True)  11.5 us
  transfers between devices with their start and end apart: 10, of which 5 were waited for; matrix products, arithmetic and copies ran while one was open for 19% of the time, Pallas kernels for 0%

commit v1 on v0

--- a/solution.py
+++ b/solution.py
@@ -17,7 +17,8 @@
 
 def over_axes(shard, axes):
     for axis in axes:
-        shard = lax.psum(shard, axis)
+        shards = lax.all_gather(shard, axis)
+        shard = jnp.sum(shards, axis=0)
     return shard
 
 

time: 410 us -> 474 us (1.16)
  local copies, waits for them, and re-layouts: 83.5 us -> 134 us
  other arithmetic: 52.8 us -> 76.2 us
  blocking collectives: 148 us -> 138 us
    psum x16 -> x0, blocking collectives: 148 us -> none  [over_axes(): shard = lax.psum(shard, axis)]
    unnamed x0 -> x16, blocking collectives: none -> 138 us
    unnamed x24 -> x114, local copies, waits for them, and re-layouts: 0.82 us -> 52.6 us
    reduce_sum x0 -> x36, other arithmetic: none -> 22.3 us  [over_axes(): shard = jnp.sum(shards, axis=0)]
  transfers between devices with their start and end apart: 10 -> 10, of which waited for: 5 -> 4; matrix products, arithmetic and copies ran while one was open for 19% -> 16% of each run, Pallas kernels for 0% -> 0%
where the time goes in v1:
time: 474 us; the launch traced here: 471 us
  blocking collectives  138 us (29%)
  local copies, waits for them, and re-layouts  134 us (28%)
  other arithmetic  76.2 us (16%)
  starting transfers between devices  44.5 us (9%)
  matrix products  43.1 us (9%)
  waiting for transfers between devices  24.3 us (5%)
  between operations  10.5 us (2%)
    unnamed x16, blocking collectives  138 us
    unnamed x114, local copies, waits for them, and re-layouts  52.6 us
    scatter x1, local copies, waits for them, and re-layouts, on_device(): jnp.zeros((partitions * capacity, 6, node_count), jnp.float32)  47.3 us
    dot_general x1, matrix products, wendland_map(): jnp.einsum('bjn,bcn->bcj', weight, force, precision=lax.Precision.HIGHEST)  42.6 us
    dot_general x4, other arithmetic, apply_operator(): jnp.einsum('abi,bi->ai', blocks[neighbor + 1], taken, precision=lax.Preci...  24.9 us
    ppermute x8, starting transfers between devices, from_behind(): return lax.ppermute(block, axis, route)  23.1 us
    all_to_all x1, waiting for transfers between devices, on_device(): lax.all_to_all(outgoing, DOM, split_axis=0, concat_axis=0, tiled=True)  22.5 us
    reduce_sum x36, other arithmetic, over_axes(): shard = jnp.sum(shards, axis=0)  22.3 us
  transfers between devices with their start and end apart: 10, of which 4 were waited for; matrix products, arithmetic and copies ran while one was open for 16% of the time, Pallas kernels for 0%

profile of v1, /device:TPU:1, one launch (start us, length us, event | category | flops | bytes accessed | tf_op | source)
XLA Modules:
  0.0 471.0 jit_solution(5969502576382814308)
XLA Ops:
  6.7 11.5 %all-to-all-start.1 = ((s32[128,1,8]{2,1,0:T(1,128)}), s32[128,1,8]{2,1,0:T(1,128)S(1)}, u32[]{:S(2)}, u32[]{:S(2)}) async-start(s32[128,1,8]{2,1,0:T(1,128)} %bitcast.41), calls=%async_computation.1 | async-start | bytes 131072 | tf_op jit(solution)/shard_map/all_to_all | solution.py:78
  22.8 47.3 %scatter_fusion = f32[1024,6,128]{2,1,0:T(8,128)} fusion(f32[1024,6,128]{2,1,0:T(8,128)} %broadcast_in_dim.40, s32[512]{0:T(512)S(1)} %bitcast.289, f32[512,6,128]{2,1,0:T(8,128)S(1)} %copy.103), kind=kCustom, calls=%fused_computation.13 | custom fusion | bytes 4720640 | tf_op jit(solution)/shard_map/scatter | solution.py:74
  74.7 9.8 %all-to-all-start = ((f32[128,8,6,128]{3,1,2,0:T(8,128)}), f32[128,8,6,128]{3,1,2,0:T(8,128)S(1)}, u32[]{:S(2)}, u32[]{:S(2)}) async-start(f32[128,8,6,128]{3,1,2,0:T(8,128)} %copy.104), calls=%async_computation | async-start | bytes 6291456 | tf_op jit(solution)/shard_map/all_to_all | solution.py:77
  87.9 8.0 %gather_fusion = f32[1024,3,32]{2,1,0:T(4,128)} fusion(f32[3,32,128]{1,0,2:T(4,128)S(1)} %copy.107, s32[1024]{0:T(1024)S(1)} %broadcast_clamp_fusion), kind=kCustom, calls=%fused_computation.12 | custom fusion | bytes 790528 | tf_op jit(solution)/shard_map/jit(_take)/gather | solution.py:81
  103.7 22.5 %all-to-all-done = f32[128,8,6,128]{3,1,2,0:T(8,128)S(1)} async-done(((f32[128,8,6,128]{3,1,2,0:T(8,128)}), f32[128,8,6,128]{3,1,2,0:T(8,128)S(1)}, u32[]{:S(2)}, u32[]{:S(2)}) %all-to-all-start) | async-done | bytes 3145760 | tf_op jit(solution)/shard_map/all_to_all | solution.py:77
  128.5 42.6 %fusion = f32[1024,3,32]{2,1,0:T(4,128)S(1)} fusion(f32[1024,128]{1,0:T(8,128)S(1)} %bitcast.282, f32[1024,32]{1,0:T(8,128)S(1)} %bitcast.280, f32[1024,128]{1,0:T(8,128)S(1)} %bitcast.283, f32[1024,32]{1,0:T(8,128)S(1)} %bitcast.279, f32[1024,128]{1,0:T(8,128)S(1)} %bitcast.281, f32[1024,32]{1,0:T(8,128)S(1)} %bitcast.278, f32[1024,6,128]{2,1,0:T(8,128)S(1)} %bitcast.263), kind=kOutput, calls=%fused_computation.15 | convolution fusion | flops 218103808 | bytes 5636096 | tf_op jit(solution)/shard_map/bjn,bcn->bcj/dot_general | solution.py:33
  184.5 6.2 %fusion.32 = (f32[128,96]{0,1:T(8,128)S(1)}, f32[128,96]{0,1:T(8,128)S(1)}, f32[128,96]{0,1:T(8,128)S(1)}) fusion(f32[3,96,96,128]{3,2,1,0:T(8,128)} %param.18, f32[128,96]{0,1:T(8,128)S(1)} %copy.236, f32[128,96]{0,1:T(8,128)S(1)} %multiply_reduce_fusion.3, f32[128,96]{0,1:T(8,128)S(1)} %copy.237), kind=kLoop, calls=%fused_computation.55 | loop fusion | flops 7041024 | bytes 14450688 | tf_op jit(solution)/shard_map/abi,bi->ai/dot_general | solution.py:49
  194.8 7.3 %all-reduce.44 = (f32[4]{0:T(128)S(1)}, f32[4]{0:T(128)S(1)}) all-reduce(f32[4]{0:T(128)S(1)} %dynamic-update-slice, f32[4]{0:T(128)S(1)} %dynamic-update-slice.4), channel_id=1, replica_groups=mesh['dom_0'=4,'dom_1'=4,'dom_2'=4,'dom_3'=2] {'dom_0'}, use_global_device_ids=true, to_apply=%add | all-reduce | flops 8 | bytes 64
  217.1 10.5 %all-reduce.38 = (f32[4]{0:T(128)S(1)}, f32[4]{0:T(128)S(1)}) all-reduce(f32[4]{0:T(128)S(1)} %dynamic-update-slice.2, f32[4]{0:T(128)S(1)} %dynamic-update-slice.6), channel_id=1, replica_groups=mesh['dom_0'=4,'dom_1'=4,'dom_2'=4,'dom_3'=2] {'dom_2'}, use_global_device_ids=true, to_apply=%add.2 | all-reduce | flops 8 | bytes 64
  231.6 9.9 %all-reduce.47 = (f32[2]{0:T(128)S(1)}, f32[2]{0:T(128)S(1)}) all-reduce(f32[2]{0:T(128)S(1)} %dynamic-update-slice.3, f32[2]{0:T(128)S(1)} %dynamic-update-slice.7), channel_id=1, replica_groups=mesh['dom_0'=4,'dom_1'=4,'dom_2'=4,'dom_3'=2] {'dom_3'}, use_global_device_ids=true, to_apply=%add.3 | all-reduce | flops 4 | bytes 32
  256.5 6.2 %fusion.33 = (f32[128,96]{0,1:T(8,128)S(1)}, f32[128,96]{0,1:T(8,128)S(1)}, f32[128,96]{0,1:T(8,128)S(1)}) fusion(f32[3,96,96,128]{3,2,1,0:T(8,128)} %param.18, f32[128,96]{0,1:T(8,128)S(1)} %copy.241, f32[128,96]{0,1:T(8,128)S(1)} %multiply_reduce_fusion.2, f32[128,96]{0,1:T(8,128)S(1)} %copy.242), kind=kLoop, calls=%fused_computation.56 | loop fusion | flops 7041024 | bytes 14450688 | tf_op jit(solution)/shard_map/abi,bi->ai/dot_general | solution.py:49
  269.1 8.6 %all-reduce.43 = (f32[4]{0:T(128)S(1)}, f32[4]{0:T(128)S(1)}, f32[4]{0:T(128)S(1)}, f32[4]{0:T(128)S(1)}) all-reduce(f32[4]{0:T(128)S(1)} %dynamic-update-slice.16, f32[4]{0:T(128)S(1)} %dynamic-update-slice.8, f32[4]{0:T(128)S(1)} %dynamic-update-slice.12, ...), channel_id=1, replica_groups=mesh['dom_0'=4,'dom_1'=4,'dom_2'=4,'dom_3'=2] {'dom_0'}, use_global_device_ids=true, to_apply=%add.16 | all-reduce | flops 16 | bytes 128
  285.8 6.0 %all-reduce.40 = (f32[4]{0:T(128)S(1)}, f32[4]{0:T(128)S(1)}, f32[4]{0:T(128)S(1)}, f32[4]{0:T(128)S(1)}) all-reduce(f32[4]{0:T(128)S(1)} %dynamic-update-slice.17, f32[4]{0:T(128)S(1)} %dynamic-update-slice.9, f32[4]{0:T(128)S(1)} %dynamic-update-slice.13, ...), channel_id=1, replica_groups=mesh['dom_0'=4,'dom_1'=4,'dom_2'=4,'dom_3'=2] {'dom_1'}, use_global_device_ids=true, to_apply=%add.17 | all-reduce | flops 16 | bytes 128
  299.4 10.8 %all-reduce.37 = (f32[4]{0:T(128)S(1)}, f32[4]{0:T(128)S(1)}, f32[4]{0:T(128)S(1)}, f32[4]{0:T(128)S(1)}) all-reduce(f32[4]{0:T(128)S(1)} %dynamic-update-slice.18, f32[4]{0:T(128)S(1)} %dynamic-update-slice.10, f32[4]{0:T(128)S(1)} %dynamic-update-slice.14, ...), channel_id=1, replica_groups=mesh['dom_0'=4,'dom_1'=4,'dom_2'=4,'dom_3'=2] {'dom_2'}, use_global_device_ids=true, to_apply=%add.18 | all-reduce | flops 16 | bytes 128
  318.1 9.4 %all-reduce.46 = (f32[2]{0:T(128)S(1)}, f32[2]{0:T(128)S(1)}, f32[2]{0:T(128)S(1)}, f32[2]{0:T(128)S(1)}) all-reduce(f32[2]{0:T(128)S(1)} %dynamic-update-slice.19, f32[2]{0:T(128)S(1)} %dynamic-update-slice.11, f32[2]{0:T(128)S(1)} %dynamic-update-slice.15, ...), channel_id=1, replica_groups=mesh['dom_0'=4,'dom_1'=4,'dom_2'=4,'dom_3'=2] {'dom_3'}, use_global_device_ids=true, to_apply=%add.19 | all-reduce | flops 8 | bytes 64
  348.2 6.2 %fusion.34 = (f32[128,96]{0,1:T(8,128)S(1)}, f32[128,96]{0,1:T(8,128)S(1)}, f32[128,96]{0,1:T(8,128)S(1)}) fusion(f32[3,96,96,128]{3,2,1,0:T(8,128)} %param.18, f32[128,96]{0,1:T(8,128)S(1)} %copy.246, f32[128,96]{0,1:T(8,128)S(1)} %multiply_reduce_fusion.1, f32[128,96]{0,1:T(8,128)S(1)} %copy.247), kind=kLoop, calls=%fused_computation.57 | loop fusion | flops 7041024 | bytes 14450688 | tf_op jit(solution)/shard_map/abi,bi->ai/dot_general | solution.py:49
  356.5 8.6 %all-reduce.24 = f32[4]{0:T(128)S(1)} all-reduce(f32[4]{0:T(128)S(1)} %dynamic-update-slice.24), channel_id=1, replica_groups=mesh['dom_0'=4,'dom_1'=4,'dom_2'=4,'dom_3'=2] {'dom_0'}, use_global_device_ids=true, to_apply=%add.24 | all-reduce | flops 4 | bytes 32
  367.1 6.2 %all-reduce.25 = f32[4]{0:T(128)S(1)} all-reduce(f32[4]{0:T(128)S(1)} %dynamic-update-slice.25), channel_id=1, replica_groups=mesh['dom_0'=4,'dom_1'=4,'dom_2'=4,'dom_3'=2] {'dom_1'}, use_global_device_ids=true, to_apply=%add.25 | all-reduce | flops 4 | bytes 32
  375.3 10.5 %all-reduce.26 = f32[4]{0:T(128)S(1)} all-reduce(f32[4]{0:T(128)S(1)} %dynamic-update-slice.26), channel_id=1, replica_groups=mesh['dom_0'=4,'dom_1'=4,'dom_2'=4,'dom_3'=2] {'dom_2'}, use_global_device_ids=true, to_apply=%add.26 | all-reduce | flops 4 | bytes 32
  387.8 9.4 %all-reduce.27 = f32[2]{0:T(128)S(1)} all-reduce(f32[2]{0:T(128)S(1)} %dynamic-update-slice.27), channel_id=1, replica_groups=mesh['dom_0'=4,'dom_1'=4,'dom_2'=4,'dom_3'=2] {'dom_3'}, use_global_device_ids=true, to_apply=%add.27 | all-reduce | flops 2 | bytes 16
  410.8 6.2 %fusion.35 = (f32[128,96]{0,1:T(8,128)S(1)}, f32[128,96]{0,1:T(8,128)S(1)}, f32[128,96]{0,1:T(8,128)S(1)}) fusion(f32[3,96,96,128]{3,2,1,0:T(8,128)} %param.18, f32[128,96]{0,1:T(8,128)S(1)} %copy.251, f32[128,96]{0,1:T(8,128)S(1)} %multiply_reduce_fusion, f32[128,96]{0,1:T(8,128)S(1)} %copy.252), kind=kLoop, calls=%fused_computation.58 | loop fusion | flops 7041024 | bytes 14450688 | tf_op jit(solution)/shard_map/abi,bi->ai/dot_general | solution.py:49
  420.6 8.6 %all-reduce.42 = (f32[4]{0:T(128)S(1)}, f32[4]{0:T(128)S(1)}) all-reduce(f32[4]{0:T(128)S(1)} %dynamic-update-slice.28, f32[4]{0:T(128)S(1)} %dynamic-update-slice.32), channel_id=1, replica_groups=mesh['dom_0'=4,'dom_1'=4,'dom_2'=4,'dom_3'=2] {'dom_0'}, use_global_device_ids=true, to_apply=%add.28 | all-reduce | flops 8 | bytes 64
  443.0 10.8 %all-reduce.36 = (f32[4]{0:T(128)S(1)}, f32[4]{0:T(128)S(1)}) all-reduce(f32[4]{0:T(128)S(1)} %dynamic-update-slice.30, f32[4]{0:T(128)S(1)} %dynamic-update-slice.34), channel_id=1, replica_groups=mesh['dom_0'=4,'dom_1'=4,'dom_2'=4,'dom_3'=2] {'dom_2'}, use_global_device_ids=true, to_apply=%add.30 | all-reduce | flops 8 | bytes 64
  457.8 9.4 %all-reduce.45 = (f32[2]{0:T(128)S(1)}, f32[2]{0:T(128)S(1)}) all-reduce(f32[2]{0:T(128)S(1)} %dynamic-update-slice.31, f32[2]{0:T(128)S(1)} %dynamic-update-slice.35), channel_id=1, replica_groups=mesh['dom_0'=4,'dom_1'=4,'dom_2'=4,'dom_3'=2] {'dom_3'}, use_global_device_ids=true, to_apply=%add.31 | all-reduce | flops 4 | bytes 32
  (259 shorter events, 167.7 us)
Async XLA Ops:
  6.7 68.0 %all-to-all-start.1 = ((s32[128,1,8]{2,1,0:T(1,128)}), s32[128,1,8]{2,1,0:T(1,128)S(1)}, u32[]{:S(2)}, u32[]{:S(2)}) async-start(s32[128,1,8]{2,1,0:T(1,128)} %bitcast.41), calls=%async_computation.1 | async-start | bytes 131072 | tf_op jit(solution)/shard_map/all_to_all | solution.py:78
  74.7 9.9 %copy-start.4 = (f32[3,32,128]{2,1,0:T(8,128)S(1)}, f32[3,32,128]{2,1,0:T(8,128)}, u32[]{:S(2)}) copy-start(f32[3,32,128]{2,1,0:T(8,128)} %param.15) | copy-start | bytes 147460
  74.7 10.0 %copy-start.9 = (s32[16]{0:T(128)S(1)}, s32[16]{0:T(128)}, u32[]{:S(2)}) copy-start(s32[16]{0:T(128)} %param.20) | copy-start | bytes 196
  74.7 10.6 %copy-start.8 = (s32[2,128]{1,0:T(2,128)S(1)}, s32[2,128]{1,0:T(2,128)}, u32[]{:S(2)}) copy-start(s32[2,128]{1,0:T(2,128)} %param.19) | copy-start | bytes 3076
  74.7 51.6 %all-to-all-start = ((f32[128,8,6,128]{3,1,2,0:T(8,128)}), f32[128,8,6,128]{3,1,2,0:T(8,128)S(1)}, u32[]{:S(2)}, u32[]{:S(2)}) async-start(f32[128,8,6,128]{3,1,2,0:T(8,128)} %copy.104), calls=%async_computation | async-start | bytes 6291456 | tf_op jit(solution)/shard_map/all_to_all | solution.py:77
  126.3 2.2 copy-start.1
  126.3 2.2 copy-start.2
  126.3 2.2 copy-start.3
  171.1 4.4 copy-start.5
  171.1 5.0 %copy-start.6 = (pred[16]{0:T(512)(128)(4,1)S(1)}, pred[16]{0:T(512)(128)(4,1)}, u32[]{:S(2)}) copy-start(pred[16]{0:T(512)(128)(4,1)} %compare_and_fusion.3) | copy-start | bytes 52
  171.1 10.6 %copy-start.7 = (s32[128]{0:T(128)S(1)}, s32[128]{0:T(128)}, u32[]{:S(2)}) copy-start(s32[128]{0:T(128)} %get-tuple-element.61) | copy-start | bytes 1540
  171.1 10.6 %copy-start.13 = (u32[128]{0:T(128)S(1)}, u32[128]{0:T(128)}, u32[]{:S(2)}) copy-start(u32[128]{0:T(128)} %constant.62) | copy-start | bytes 1540
  172.3 226.2 %copy-start = (f32[96,128]{1,0:T(8,128)}, f32[96,128]{1,0:T(8,128)S(1)}, u32[]{:S(2)}) copy-start(f32[96,128]{1,0:T(8,128)S(1)} %fusion.41) | copy-start | bytes 147460
  176.2 6.3 %collective-permute-start.1 = (f32[96,16]{0,1:T(8,128)S(1)}, f32[96,16]{0,1:T(8,128)S(1)}, u32[]{:S(2)}, u32[]{:S(2)}) collective-permute-start(f32[96,16]{0,1:T(8,128)S(1)} %select_bitcast_fusion.3), channel_id=1, source_target_pairs={{1,0},{2,1},{3,2},{4,3},{5,4},{6,5},{7,6},{8,7},{9,8},{10,9},{11,1... | collective-permute-start | bytes 18440 | tf_op jit(solution)/shard_map/ppermute | solution.py:15
  179.2 3.3 collective-permute-start
  184.5 9.8 %copy-start.12 = (u32[128]{0:T(128)S(1)}, u32[128]{0:T(128)}, u32[]{:S(2)}) copy-start(u32[128]{0:T(128)} %constant.67) | copy-start | bytes 1540
  184.5 21.6 %copy-start.11 = (u32[128]{0:T(128)S(1)}, u32[128]{0:T(128)}, u32[]{:S(2)}) copy-start(u32[128]{0:T(128)} %constant.72) | copy-start | bytes 1540
  184.5 32.0 %copy-start.10 = (u32[128]{0:T(128)S(1)}, u32[128]{0:T(128)}, u32[]{:S(2)}) copy-start(u32[128]{0:T(128)} %constant.77) | copy-start | bytes 1540
  248.0 5.8 %collective-permute-start.3 = (f32[96,16]{0,1:T(8,128)S(1)}, f32[96,16]{0,1:T(8,128)S(1)}, u32[]{:S(2)}, u32[]{:S(2)}) collective-permute-start(f32[96,16]{0,1:T(8,128)S(1)} %select_bitcast_fusion.2), channel_id=1, source_target_pairs={{1,0},{2,1},{3,2},{4,3},{5,4},{6,5},{7,6},{8,7},{9,8},{10,9},{11,1... | collective-permute-start | bytes 18440 | tf_op jit(solution)/shard_map/ppermute | solution.py:15
  250.3 4.3 collective-permute-start.2
  339.7 5.8 %collective-permute-start.5 = (f32[96,16]{0,1:T(8,128)S(1)}, f32[96,16]{0,1:T(8,128)S(1)}, u32[]{:S(2)}, u32[]{:S(2)}) collective-permute-start(f32[96,16]{0,1:T(8,128)S(1)} %select_bitcast_fusion.1), channel_id=1, source_target_pairs={{1,0},{2,1},{3,2},{4,3},{5,4},{6,5},{7,6},{8,7},{9,8},{10,9},{11,1... | collective-permute-start | bytes 18440 | tf_op jit(solution)/shard_map/ppermute | solution.py:15
  341.9 4.3 collective-permute-start.4
  402.4 6.1 %collective-permute-start.7 = (f32[96,16]{0,1:T(8,128)S(1)}, f32[96,16]{0,1:T(8,128)S(1)}, u32[]{:S(2)}, u32[]{:S(2)}) collective-permute-start(f32[96,16]{0,1:T(8,128)S(1)} %select_bitcast_fusion), channel_id=1, source_target_pairs={{1,0},{2,1},{3,2},{4,3},{5,4},{6,5},{7,6},{8,7},{9,8},{10,9},{11,1... | collective-permute-start | bytes 18440 | tf_op jit(solution)/shard_map/ppermute | solution.py:15
  404.6 4.3 collective-permute-start.6
